TPU v7x, 256 devices: a whole 4x4x8 slice. The times are simulated.
256 devices in a mesh: dom: 64 (over z, x, core), tp: 4 (over y).
Axes of the slice: x: 4, y: 4, z: 8, core: 2. Of those that a mesh axis runs over, the one named last changes fastest.
Arguments:
- state: bfloat16 [2, 65536, 512], P(None, 'dom'), may hold values from -6 to 6
- norm_gain: float32 [2, 2, 512], replicated, may hold values from 0.1 to 1.9
- norm_shift: float32 [2, 2, 512], replicated, may hold values from -3 to 3
- qkv_weight: bfloat16 [512, 3, 512], P(None, None, 'tp'), may hold values from -0.5 to 0.5
- out_weight: bfloat16 [512, 512], P('tp'), may hold values from -0.25 to 0.25
- up_weight: bfloat16 [512, 2048], P(None, 'tp'), may hold values from -0.25 to 0.25
- down_weight: bfloat16 [2048, 512], P('tp'), may hold values from -0.125 to 0.125
- neighbours: int32 [512, 8], P('dom'), may hold values from 0 to 511, as said below
- counts: int32 [512], P('dom'), may hold values from 2 to 8, as said below
Outputs:
- layer_out: bfloat16 [2, 65536, 512], P(None, 'dom', 'tp')
Inputs may be any that keep to these rules, and one draw needn't show every extreme that they name: `neighbours`: entry 0 of row b is b itself; the other 7 entries are distinct blocks whose partition (block // 8) lies at most two partitions before or after b's on a closed chain of partitions, block numbers taken modulo 512. `counts`: every partition has a block whose count is 8.
All inputs are finite; a program needn't handle non-finite values.
Results may differ from a plain program's by a relative error of at most 0.017.
Values may be sent and summed in bfloat16 or wider, within the bound.
No kernel may reach another device: no remote copies, remote signals or barrier semaphores. Data moves between devices by JAX's collectives and lax.ppermute only.
A program may use at most 64 MiB of HBM per device.

v0:
```python
import math
import jax
import jax.numpy as jnp
from jax import lax
from jax.sharding import PartitionSpec as P

HEADS = 4
NODE_BLK = 128
KMAX = 8


def with_halo(value, sides, width):
    for axis, dim in sides:
        peers, length = (lax.axis_size(axis), value.shape[dim])
        up = [(i, (i + 1) % peers) for i in range(peers)]
        down = [(j, i) for i, j in up]
        last = lax.slice_in_dim(value, length - width, length, axis=dim)
        leading = lax.slice_in_dim(value, 0, width, axis=dim)
        before = lax.ppermute(last, axis, up)
        after = lax.ppermute(leading, axis, down)
        value = jnp.concatenate([before, value, after], axis=dim)
    return value


def shifted(block, axis, distance):
    devices = range(lax.axis_size(axis))
    route = [((i - distance) % len(devices), i) for i in devices]
    return lax.ppermute(block, axis, route)


def layer_norm(values, gain_row, shift_row):
    row_mean = jnp.mean(values, axis=-1, keepdims=True)
    centred = values - row_mean
    spread = jnp.mean(centred * centred, axis=-1, keepdims=True)
    return centred * lax.rsqrt(spread + 1e-05) * gain_row + shift_row


def local(
    state, norm_gain, norm_shift, qkv_weight, out_weight, up_weight, down_weight, neighbours, counts
):
    samples, row_count, feat_width = state.shape
    per_dev = row_count // NODE_BLK
    block_count = per_dev * lax.axis_size("dom")
    head_cols = qkv_weight.shape[2]
    head_size = feat_width // HEADS
    heads_here = head_cols // head_size
    tp_rank = lax.axis_index("tp")
    resid_in = state.astype(jnp.float32)
    normed = layer_norm(resid_in, norm_gain[0][:, None, :], norm_shift[0][:, None, :]).astype(
        jnp.bfloat16
    )
    normed = normed.reshape(samples, per_dev, NODE_BLK, feat_width)
    projected = jnp.einsum(
        "sbnd,dce->bsnce", normed, qkv_weight, preferred_element_type=jnp.float32
    ).astype(jnp.bfloat16)
    query_heads = projected[:, :, :, 0].reshape(per_dev, samples, NODE_BLK, heads_here, head_size)
    own_pairs = projected[:, :, :, 1:].reshape(per_dev, samples, NODE_BLK, 2 * head_cols)
    near_side = with_halo(own_pairs, (("dom", 0),), per_dev)
    far_side = [shifted(own_pairs, "dom", offset) for offset in (2, -2)]
    window = jnp.concatenate([far_side[0], near_side, far_side[1]], axis=0)
    first_block = lax.axis_index("dom") * per_dev - 2 * per_dev
    window_idx = jnp.mod(neighbours - first_block, block_count)
    chosen = window[window_idx]
    key_rows = chosen[..., :head_cols].reshape(
        per_dev, KMAX, samples, NODE_BLK, heads_here, head_size
    )
    value_rows = chosen[..., head_cols:].reshape(
        per_dev, KMAX, samples, NODE_BLK, heads_here, head_size
    )
    scores = jnp.einsum(
        "bsqhe,bjskhe->bshqjk", query_heads, key_rows, preferred_element_type=jnp.float32
    ) / math.sqrt(head_size)
    live_mask = jnp.arange(KMAX, dtype=jnp.int32)[None, :] < counts[:, None]
    masked = jnp.where(live_mask[:, None, None, None, :, None], scores, -1e30)
    row_top = jnp.max(masked, axis=(4, 5), keepdims=True)
    weights = jnp.exp(masked - row_top)
    weights = (weights / jnp.sum(weights, axis=(4, 5), keepdims=True)).astype(jnp.bfloat16)
    mixed_heads = jnp.einsum(
        "bshqjk,bjskhe->sbqhe", weights, value_rows, preferred_element_type=jnp.float32
    ).astype(jnp.bfloat16)
    mixed_heads = mixed_heads.reshape(samples, row_count, head_cols)
    partial_value = jnp.einsum(
        "sre,ed->srd", mixed_heads, out_weight, preferred_element_type=jnp.float32
    )
    attn_sum = lax.psum(partial_value.astype(jnp.bfloat16), "tp").astype(jnp.float32)
    residual = resid_in + attn_sum
    normed2 = layer_norm(residual, norm_gain[1][:, None, :], norm_shift[1][:, None, :]).astype(
        jnp.bfloat16
    )
    hidden = jax.nn.silu(
        jnp.einsum("srd,df->srf", normed2, up_weight, preferred_element_type=jnp.float32)
    ).astype(jnp.bfloat16)
    update = jnp.einsum("srf,fd->srd", hidden, down_weight, preferred_element_type=jnp.float32)
    update = lax.psum_scatter(
        update.astype(jnp.bfloat16), "tp", scatter_dimension=2, tiled=True
    ).astype(jnp.float32)
    col_share = update.shape[2]
    kept_cols = lax.dynamic_slice_in_dim(residual, tp_rank * col_share, col_share, 2)
    return (kept_cols + update).astype(jnp.bfloat16)


def solution(mesh):
    placed = (
        P(None, "dom", None),
        P(),
        P(),
        P(None, None, "tp"),
        P("tp", None),
        P(None, "tp"),
        P("tp", None),
        P("dom", None),
        P("dom"),
    )
    return jax.shard_map(
        local, mesh=mesh, in_specs=placed, out_specs=P(None, "dom", "tp"), check_vma=False
    )
```

profile of v0, /device:TPU:1, one launch (start us, length us, event | category | flops | bytes accessed | tf_op | source)
XLA Modules:
  0.0 212.8 jit_solution(13900519222820151107)
XLA Ops:
  6.5 0.0 copy-start
  6.5 0.0 copy-start.1
  6.5 0.0 copy-start.6
  6.5 0.0 copy-start.7
  6.5 0.0 copy-start.10
  6.5 0.0 all-reduce.2.cloned.1.call-start
  6.6 2.1 convert_reduce_fusion
  8.7 2.4 %fusion.4 = f32[2,1024]{1,0:T(2,128)S(1)} fusion(bf16[2,1024,512]{2,1,0:T(8,128)(2,1)} %param.9, f32[2,1024]{1,0:T(2,128)S(1)} %broadcast_multiply_fusion.1), kind=kLoop, calls=%fused_computation.11 | loop fusion | flops 4192256 | bytes 2113536 | tf_op jit(solution)/shard_map/reduce_sum | solution.py:34
  11.2 0.0 copy-done.6
  11.2 0.0 copy-done.7
  11.2 0.0 copy-done.1
  11.2 0.9 fusion.7
  12.2 0.0 copy-done.10
  12.2 0.0 copy-start.8
  12.2 0.0 copy-start.11
  12.2 1.0 fusion.20
  13.2 0.0 copy-start.4
  13.2 1.1 copy-done.4
  14.4 1.1 slice.34
  15.5 2.3 %copy.30 = bf16[8,2,128,256]{3,2,1,0:T(8,128)(2,1)} copy(bf16[8,2,128,256]{2,3,0,1:T(8,128)(2,1)} %bitcast.55) | data formatting | bytes 2097152 | tf_op jit(solution)/shard_map/reshape | solution.py:57
  17.7 2.0 collective-permute-start
  19.8 2.1 collective-permute-start.1
  21.8 0.0 collective-permute-start.2
  21.8 5.3 %collective-permute-start.3 = (bf16[8,2,128,256]{3,2,1,0:T(8,128)(2,1)}, bf16[8,2,128,256]{3,2,1,0:T(8,128)(2,1)}, u32[]{:S(2)}, u32[]{:S(2)}) collective-permute-start(bf16[8,2,128,256]{3,2,1,0:T(8,128)(2,1)} %copy.30), channel_id=1, source_target_pairs={{8,0},{12,4},{16,8},{20,12},{24,16},{28,20},{32,24},{36,28},{40,32... | collective-permute-start | bytes 3145736 | tf_op jit(solution)/shard_map/ppermute | solution.py:28
  27.1 0.0 copy-done.8
  27.1 0.1 reshape.95
  27.2 0.0 copy-start.3
  27.2 0.0 copy-done.11
  27.2 0.1 iota_compare_fusion
  27.3 22.3 %collective-permute-done = bf16[8,2,128,256]{3,2,1,0:T(8,128)(2,1)} collective-permute-done((bf16[8,2,128,256]{3,2,1,0:T(8,128)(2,1)}, bf16[8,2,128,256]{3,2,1,0:T(8,128)(2,1)}, u32[]{:S(2)}, u32[]{:S(2)}) %collective-permute-start) | collective-permute-done | bytes 1048608 | tf_op jit(solution)/shard_map/ppermute | solution.py:28
  49.5 2.4 %constant_dynamic-update-slice_fusion.4 = bf16[40,2,128,256]{3,2,1,0:T(8,128)(2,1)} fusion(bf16[8,2,128,256]{3,2,1,0:T(8,128)(2,1)} %collective-permute-done), kind=kLoop, calls=%fused_computation.47 | loop fusion | bytes 2097152
  51.9 2.4 %collective-permute-done.1 = bf16[8,2,128,256]{3,2,1,0:T(8,128)(2,1)} collective-permute-done((bf16[8,2,128,256]{3,2,1,0:T(8,128)(2,1)}, bf16[8,2,128,256]{3,2,1,0:T(8,128)(2,1)}, u32[]{:S(2)}, u32[]{:S(2)}) %collective-permute-start.1) | collective-permute-done | bytes 1048608 | tf_op jit(solution)/shard_map/ppermute | solution.py:19
  54.3 2.3 %constant_dynamic-update-slice_fusion.3 = bf16[40,2,128,256]{3,2,1,0:T(8,128)(2,1)} fusion(bf16[40,2,128,256]{3,2,1,0:T(8,128)(2,1)} %constant_dynamic-update-slice_fusion.4, bf16[8,2,128,256]{3,2,1,0:T(8,128)(2,1)} %collective-permute-done.1), kind=kLoop, calls=%fused_computation.46 | loop fusion | bytes 2097152
  56.6 0.0 copy-done.3
  56.6 1.0 constant_dynamic-update-slice_fusion.2
  57.6 0.0 collective-permute-done.2
  57.6 2.3 %constant_dynamic-update-slice_fusion.1 = bf16[40,2,128,256]{3,2,1,0:T(8,128)(2,1)} fusion(bf16[40,2,128,256]{3,2,1,0:T(8,128)(2,1)} %constant_dynamic-update-slice_fusion.2, bf16[8,2,128,256]{3,2,1,0:T(8,128)(2,1)} %collective-permute-done.2), kind=kLoop, calls=%fused_computation.44 | loop fusion | bytes 2097152
  59.9 0.0 collective-permute-done.3
  59.9 2.4 %constant_dynamic-update-slice_fusion = bf16[40,2,128,256]{3,2,1,0:T(8,128)(2,1)} fusion(bf16[40,2,128,256]{3,2,1,0:T(8,128)(2,1)} %constant_dynamic-update-slice_fusion.1, bf16[8,2,128,256]{3,2,1,0:T(8,128)(2,1)} %collective-permute-done.3), kind=kLoop, calls=%fused_computation.43 | loop fusion | bytes 2097152 | tf_op jit(solution)/shard_map/concatenate | solution.py:60
  62.3 8.0 %gather_fusion = bf16[64,2,128,256]{3,2,1,0:T(8,128)(2,1)} fusion(bf16[40,2,128,256]{3,2,1,0:T(8,128)(2,1)} %constant_dynamic-update-slice_fusion, s32[1024]{0:T(1024)S(1)} %pad_clamp_fusion), kind=kCustom, calls=%fused_computation | custom fusion | bytes 16777472 | tf_op jit(solution)/shard_map/gather | solution.py:63
  70.3 3.8 %fusion.40 = (bf16[8,8,2,128,128]{4,3,2,1,0:T(8,128)(2,1)S(1)}, bf16[8,8,2,128,128]{4,3,2,1,0:T(8,128)(2,1)S(1)}) fusion(bf16[8,8,2,128,256]{4,3,2,1,0:T(8,128)(2,1)} %bitcast.52), kind=kLoop, calls=%fused_computation.64 | loop fusion | bytes 16777216 | tf_op jit(solution)/shard_map/slice | solution.py:67
  74.1 2.4 %fusion = (f32[8,2,128]{2,1,0:T(2,128)S(1)}, f32[8,2,128,8,128]{2,4,3,1,0:T(8,128)S(1)}) fusion(pred[8,8]{1,0:T(8,128)(4,1)S(1)} %iota_compare_fusion, bf16[8,8,2,128,128]{4,3,2,1,0:T(8,128)(2,1)S(1)} %get-tuple-element.6, bf16[8,2,128,3,128]{2,4,3,0,1:T(8,128)(2,1)} %copy-done.4), kind=kOutput, calls=%fused_computation.4 | convolution fusion | flops 543160320 | bytes 13115456 | tf_op jit(solution)/shard_map/bsqhe,bjskhe->bshqjk/dot_general | solution.py:70
  76.5 2.0 fusion.1
  78.5 0.0 copy-start.5
  78.5 2.8 %fusion.26 = bf16[2,8,128,128]{2,3,1,0:T(8,128)(2,1)S(1)} fusion(bf16[8,8,2,128,128]{4,3,2,1,0:T(8,128)(2,1)S(1)} %get-tuple-element.5, f32[8,2,128,8,128]{2,4,3,1,0:T(8,128)S(1)} %get-tuple-element.14, f32[8,2,128]{2,1,0:T(2,128)S(1)} %fusion.1, f32[8,2,128]{2,1,0:T(2,128)S(1)} %get-tuple-element.13, pred[8,8]{1,0:T(8,128)(4,1)S(1)} %iota_compare_fusion), kind=kOutput, calls=%fused_computation.34 | convolution fusion | flops 547618816 | bytes 13123648 | tf_op jit(solution)/shard_map/bshqjk,bjskhe->sbqhe/dot_general | solution.py:78
  81.3 0.0 copy-done.5
  81.3 2.0 convolution_convert_fusion
  83.3 0.0 all-reduce.2.cloned.1.call-update
  83.4 0.0 reduce-scatter.4.cloned.1.call-start
  83.4 68.5 %all-reduce.2.cloned.1.call-done = bf16[2,1024,512]{2,1,0:T(8,128)(2,1)} async-done(((bf16[2,1024,512]{2,1,0:T(8,128)(2,1)}), bf16[2,1024,512]{2,1,0:T(8,128)(2,1)}) %all-reduce.2.cloned.1.call-update) | async-done | bytes 2097168 | tf_op jit(solution)/shard_map/psum | solution.py:85
  151.9 0.0 copy-start.2
  151.9 4.2 %convert_add_fusion = (f32[2,1024,512]{2,1,0:T(8,128)}, f32[2,1024]{1,0:T(2,128)S(1)}) fusion(bf16[2,1024,512]{2,1,0:T(8,128)(2,1)S(1)} %copy-done.1, bf16[2,1024,512]{2,1,0:T(8,128)(2,1)} %all-reduce.2.cloned.1.call-done), kind=kLoop, calls=%fused_computation.6 | loop fusion | flops 4192256 | bytes 8396800 | tf_op jit(solution)/shard_map/add | solution.py:86
  156.1 0.0 copy-done.2
  156.1 1.0 multiply_reduce_fusion
  157.2 0.0 copy-done
  157.2 0.0 copy-done.9
  157.2 5.5 %fusion.19 = bf16[2,1024,512]{2,1,0:T(8,128)(2,1)} fusion(f32[2,512]{1,0:T(2,128)S(1)} %get-tuple-element.12, f32[2,512]{1,0:T(2,128)S(1)} %get-tuple-element.15, f32[2,1024]{1,0:T(2,128)S(1)} %add_rsqrt_fusion, f32[2,1024]{1,0:T(2,128)S(1)} %broadcast_multiply_fusion, bf16[512,512]{1,0:T(8,128)(2,1)S(1)} %copy-done, bf16[512,512]{1,0:T(8,128)(2,1)S(1)} %copy-done.9, ...), kind=kOutput, calls=%fused_computation.29 | convolution fusion | flops 2162163712 | bytes 7364608 | tf_op jit(solution)/shard_map/srf,fd->srd/dot_general | solution.py:93
  162.6 5.0 %copy.48 = bf16[2,1024,512]{1,0,2:T(2,128)(2,1)S(1)} copy(bf16[2,1024,512]{2,1,0:T(8,128)(2,1)} %fusion.19) | data formatting | bytes 4194304
  167.7 1.9 copy.52
  169.6 0.0 reduce-scatter.4.cloned.1.call-update
  169.6 32.3 %reduce-scatter.4.cloned.1.call-done = bf16[128,2048]{1,0:T(8,128)(2,1)} async-done(((bf16[512,2048]{1,0:T(8,128)(2,1)}), bf16[128,2048]{1,0:T(8,128)(2,1)}) %reduce-scatter.4.cloned.1.call-update) | async-done | bytes 524304
  201.9 1.4 reshape.111
  203.3 0.5 copy.49
  203.9 2.1 %add_convert_fusion.6 = bf16[2,1024,128]{2,1,0:T(8,128)(2,1)} fusion(bf16[2,1024,128]{2,1,0:T(8,128)(2,1)S(1)} %copy.49, f32[2,1024,512]{2,1,0:T(8,128)} %get-tuple-element.7, s32[]{:T(128)S(6)} %select_n.21), kind=kLoop, calls=%fused_computation.35 | loop fusion | flops 786432 | bytes 2097156 | tf_op jit(solution)/shard_map/convert_element_type | solution.py:99
  (8 shorter events, 0.1 us)
Async XLA Ops:
  6.5 150.6 %copy-start = (bf16[512,512]{1,0:T(8,128)(2,1)S(1)}, bf16[512,512]{1,0:T(8,128)(2,1)}, u32[]{:S(2)}) copy-start(bf16[512,512]{1,0:T(8,128)(2,1)} %param.15) | copy-start | bytes 1572868
  6.5 4.7 %copy-start.1 = (bf16[2,1024,512]{2,1,0:T(8,128)(2,1)S(1)}, bf16[2,1024,512]{2,1,0:T(8,128)(2,1)}, u32[]{:S(2)}) copy-start(bf16[2,1024,512]{2,1,0:T(8,128)(2,1)} %param.9) | copy-start | bytes 6291460
  6.5 4.6 %copy-start.6 = (f32[2,2,512]{2,1,0:T(2,128)S(1)}, f32[2,2,512]{2,1,0:T(2,128)}, u32[]{:S(2)}) copy-start(f32[2,2,512]{2,1,0:T(2,128)} %param.11) | copy-start | bytes 24580
  6.5 4.6 %copy-start.7 = (f32[2,2,512]{2,1,0:T(2,128)S(1)}, f32[2,2,512]{2,1,0:T(2,128)}, u32[]{:S(2)}) copy-start(f32[2,2,512]{2,1,0:T(2,128)} %param.10) | copy-start | bytes 24580
  6.5 5.6 %copy-start.10 = (bf16[512,3,128]{2,0,1:T(8,128)(2,1)S(1)}, bf16[512,3,128]{2,0,1:T(8,128)(2,1)}, u32[]{:S(2)}) copy-start(bf16[512,3,128]{2,0,1:T(8,128)(2,1)} %param.12) | copy-start | bytes 1179652
  6.5 145.4 %all-reduce.2.cloned.1.call-start = ((), (), s32[]{:S(2)}) async-start(), calls=%async_computation.1 | async-start | bytes 4194304 | tf_op jit(solution)/shard_map/psum | solution.py:85
  12.2 14.9 %copy-start.8 = (s32[8,8]{1,0:T(8,128)S(1)}, s32[8,8]{1,0:T(8,128)}, u32[]{:S(2)}) copy-start(s32[8,8]{1,0:T(8,128)} %param.16) | copy-start | bytes 772
  12.2 15.0 %copy-start.11 = (s32[8]{0:T(128)S(1)}, s32[8]{0:T(128)}, u32[]{:S(2)}) copy-start(s32[8]{0:T(128)} %param.17) | copy-start | bytes 100
  13.2 1.2 copy-start.4
  17.7 31.8 %collective-permute-start = (bf16[8,2,128,256]{3,2,1,0:T(8,128)(2,1)}, bf16[8,2,128,256]{3,2,1,0:T(8,128)(2,1)}, u32[]{:S(2)}, u32[]{:S(2)}) collective-permute-start(bf16[8,2,128,256]{3,2,1,0:T(8,128)(2,1)} %copy.30), channel_id=1, source_target_pairs={{248,0},{252,4},{0,8},{4,12},{8,16},{12,20},{16,24},{20,28},{24,32... | collective-permute-start | bytes 3145736 | tf_op jit(solution)/shard_map/ppermute | solution.py:28
  19.8 34.5 %collective-permute-start.1 = (bf16[8,2,128,256]{3,2,1,0:T(8,128)(2,1)}, bf16[8,2,128,256]{3,2,1,0:T(8,128)(2,1)}, u32[]{:S(2)}, u32[]{:S(2)}) collective-permute-start(bf16[8,2,128,256]{3,2,1,0:T(8,128)(2,1)} %copy.30), channel_id=1, source_target_pairs={{0,4},{4,8},{8,12},{12,16},{16,20},{20,24},{24,28},{28,32},{32,36}... | collective-permute-start | bytes 3145736 | tf_op jit(solution)/shard_map/ppermute | solution.py:19
  21.8 35.8 %collective-permute-start.2 = (bf16[8,2,128,256]{3,2,1,0:T(8,128)(2,1)}, bf16[8,2,128,256]{3,2,1,0:T(8,128)(2,1)}, u32[]{:S(2)}, u32[]{:S(2)}) collective-permute-start(bf16[8,2,128,256]{3,2,1,0:T(8,128)(2,1)} %copy.30), channel_id=1, source_target_pairs={{4,0},{8,4},{12,8},{16,12},{20,16},{24,20},{28,24},{32,28},{36,32}... | collective-permute-start | bytes 3145736 | tf_op jit(solution)/shard_map/ppermute | solution.py:20
  21.8 38.1 %collective-permute-start.3 = (bf16[8,2,128,256]{3,2,1,0:T(8,128)(2,1)}, bf16[8,2,128,256]{3,2,1,0:T(8,128)(2,1)}, u32[]{:S(2)}, u32[]{:S(2)}) collective-permute-start(bf16[8,2,128,256]{3,2,1,0:T(8,128)(2,1)} %copy.30), channel_id=1, source_target_pairs={{8,0},{12,4},{16,8},{20,12},{24,16},{28,20},{32,24},{36,28},{40,32... | collective-permute-start | bytes 3145736 | tf_op jit(solution)/shard_map/ppermute | solution.py:28
  27.2 29.4 %copy-start.3 = (bf16[8,2,128,256]{3,2,1,0:T(8,128)(2,1)S(1)}, bf16[8,2,128,256]{3,2,1,0:T(8,128)(2,1)}, u32[]{:S(2)}) copy-start(bf16[8,2,128,256]{3,2,1,0:T(8,128)(2,1)} %copy.30) | copy-start | bytes 3145732
  78.5 2.8 %copy-start.5 = (bf16[128,512]{1,0:T(8,128)(2,1)S(1)}, bf16[128,512]{1,0:T(8,128)(2,1)}, u32[]{:S(2)}) copy-start(bf16[128,512]{1,0:T(8,128)(2,1)} %param.13) | copy-start | bytes 393220
  83.4 118.6 %reduce-scatter.4.cloned.1.call-start = ((), (), s32[]{:S(2)}) async-start(), calls=%async_computation.2 | async-start | bytes 2621440
  151.9 4.2 %copy-start.2 = (bf16[2,1024,512]{2,1,0:T(8,128)(2,1)S(1)}, bf16[2,1024,512]{2,1,0:T(8,128)(2,1)}, u32[]{:S(2)}) copy-start(bf16[2,1024,512]{2,1,0:T(8,128)(2,1)} %all-reduce.2.cloned.1.call-done) | copy-start | bytes 6291460
  156.1 1.0 copy-start.9
Sparse Core Ops, SparseCore 0:
  83.5 68.3 all-reduce.1
  169.8 32.1 reduce-scatter.3
where the time goes:
time: 213 us
  waiting for transfers between devices  125 us (59%)
  local copies, waits for them, and re-layouts  35.7 us (17%)
  other arithmetic  14.9 us (7%)
  matrix products  13.7 us (6%)
  between operations  13.6 us (6%)
  starting transfers between devices  9.43 us (4%)
    psum x1, waiting for transfers between devices, local(): lax.psum(partial_value.astype(jnp.bfloat16), 'tp').astype(jnp.float32)  68.5 us
    unnamed x3, waiting for transfers between devices  32.3 us
    ppermute x2, waiting for transfers between devices, shifted(): return lax.ppermute(block, axis, route)  22.3 us
    unnamed x32, local copies, waits for them, and re-layouts  18.1 us
    gather x1, local copies, waits for them, and re-layouts, local(): chosen = window[window_idx]  8.02 us
    ppermute x2, starting transfers between devices, shifted(): return lax.ppermute(block, axis, route)  7.3 us
    dot_general x1, matrix products, local(): jnp.einsum('srf,fd->srd', hidden, down_weight, preferred_element_type=jnp...  5.48 us
  transfers between devices with their start and end apart: 6, of which 4 were waited for; matrix products, arithmetic and copies ran while one was open for 4% of the time, Pallas kernels for 0%

commit v1 on v0

--- a/solution.py
+++ b/solution.py
@@ -82,7 +82,9 @@
     partial_value = jnp.einsum(
         "sre,ed->srd", mixed_heads, out_weight, preferred_element_type=jnp.float32
     )
-    attn_sum = lax.psum(partial_value.astype(jnp.bfloat16), "tp").astype(jnp.float32)
+    attn_sum = jnp.sum(lax.all_gather(partial_value.astype(jnp.bfloat16), "tp"), axis=0).astype(
+        jnp.float32
+    )
     residual = resid_in + attn_sum
     normed2 = layer_norm(residual, norm_gain[1][:, None, :], norm_shift[1][:, None, :]).astype(
         jnp.bfloat16

time: 213 us -> 243 us (1.14)
  waiting for transfers between devices: 125 us -> 148 us
  other arithmetic: 14.9 us -> 21.6 us
    all_gather x0 -> x1, waiting for transfers between devices: none -> 90.1 us  [local(): lax.all_gather(partial_value.astype(jnp.bfloat16), 'tp')]
    psum x1 -> x0, waiting for transfers between devices: 68.5 us -> none  [local(): lax.psum(partial_value.astype(jnp.bfloat16), 'tp').astype(jnp.float32)]
    reduce_sum x0 -> x1, other arithmetic: none -> 6.69 us  [local(): jnp.sum(lax.all_gather(partial_value.astype(jnp.bfloat16), 'tp'), axis=0)]
  transfers between devices with their start and end apart: 6 -> 6, of which waited for: 4 -> 4; matrix products, arithmetic and copies ran while one was open for 4% -> 3% of each run, Pallas kernels for 0% -> 0%
where the time goes in v1:
time: 243 us
  waiting for transfers between devices  148 us (61%)
  local copies, waits for them, and re-layouts  35.7 us (15%)
  other arithmetic  21.6 us (9%)
  matrix products  13.7 us (6%)
  between operations  13.6 us (6%)
  starting transfers between devices  9.65 us (4%)
    all_gather x1, waiting for transfers between devices, local(): lax.all_gather(partial_value.astype(jnp.bfloat16), 'tp')  90.1 us
    unnamed x3, waiting for transfers between devices  33.5 us
    ppermute x2, waiting for transfers between devices, shifted(): return lax.ppermute(block, axis, route)  22.3 us
    unnamed x32, local copies, waits for them, and re-layouts  18.1 us
    gather x1, local copies, waits for them, and re-layouts, local(): chosen = window[window_idx]  8.02 us
    ppermute x2, starting transfers between devices, shifted(): return lax.ppermute(block, axis, route)  7.3 us
    reduce_sum x1, other arithmetic, local(): jnp.sum(lax.all_gather(partial_value.astype(jnp.bfloat16), 'tp'), axis=0)  6.69 us
    dot_general x1, matrix products, local(): jnp.einsum('srf,fd->srd', hidden, down_weight, preferred_element_type=jnp...  5.49 us
  transfers between devices with their start and end apart: 6, of which 4 were waited for; matrix products, arithmetic and copies ran while one was open for 3% of the time, Pallas kernels for 0%

profile of v1, /device:TPU:1, one launch (start us, length us, event | category | flops | bytes accessed | tf_op | source)
XLA Modules:
  0.0 242.6 jit_solution(14445024564983074336)
XLA Ops:
  6.5 0.0 copy-start
  6.5 0.0 copy-start.1
  6.5 0.0 copy-start.6
  6.5 0.0 copy-start.7
  6.5 0.0 copy-start.10
  6.5 0.0 all-gather.3.cloned.1.call-start
  6.6 2.1 convert_reduce_fusion
  8.7 2.4 %fusion.4 = f32[2,1024]{1,0:T(2,128)S(1)} fusion(bf16[2,1024,512]{2,1,0:T(8,128)(2,1)} %param.9, f32[2,1024]{1,0:T(2,128)S(1)} %broadcast_multiply_fusion.1), kind=kLoop, calls=%fused_computation.11 | loop fusion | flops 4192256 | bytes 2113536 | tf_op jit(solution)/shard_map/reduce_sum | solution.py:34
  11.2 0.0 copy-done.6
  11.2 0.0 copy-done.7
  11.2 0.0 copy-done.1
  11.2 0.9 fusion.7
  12.2 0.0 copy-done.10
  12.2 0.0 copy-start.8
  12.2 0.0 copy-start.11
  12.2 1.0 fusion.20
  13.2 0.0 copy-start.4
  13.2 1.1 copy-done.4
  14.4 1.1 slice.34
  15.5 2.3 copy.30
  17.7 2.0 collective-permute-start
  19.8 2.1 collective-permute-start.1
  21.8 0.0 collective-permute-start.2
  21.8 5.3 %collective-permute-start.3 = (bf16[8,2,128,256]{3,2,1,0:T(8,128)(2,1)}, bf16[8,2,128,256]{3,2,1,0:T(8,128)(2,1)}, u32[]{:S(2)}, u32[]{:S(2)}) collective-permute-start(bf16[8,2,128,256]{3,2,1,0:T(8,128)(2,1)} %copy.30), channel_id=1, source_target_pairs={{8,0},{12,4},{16,8},{20,12},{24,16},{28,20},{32,24},{36,28},{40,32... | collective-permute-start | bytes 3145736 | tf_op jit(solution)/shard_map/ppermute | solution.py:28
  27.1 0.0 copy-done.8
  27.1 0.1 reshape.95
  27.2 0.0 copy-start.3
  27.2 0.0 copy-done.11
  27.2 0.1 iota_compare_fusion
  27.3 22.3 %collective-permute-done = bf16[8,2,128,256]{3,2,1,0:T(8,128)(2,1)} collective-permute-done((bf16[8,2,128,256]{3,2,1,0:T(8,128)(2,1)}, bf16[8,2,128,256]{3,2,1,0:T(8,128)(2,1)}, u32[]{:S(2)}, u32[]{:S(2)}) %collective-permute-start) | collective-permute-done | bytes 1048608 | tf_op jit(solution)/shard_map/ppermute | solution.py:28
  49.5 2.4 constant_dynamic-update-slice_fusion.4
  51.9 2.4 collective-permute-done.1
  54.3 2.3 constant_dynamic-update-slice_fusion.3
  56.6 0.0 copy-done.3
  56.6 1.0 constant_dynamic-update-slice_fusion.2
  57.6 0.0 collective-permute-done.2
  57.6 2.3 constant_dynamic-update-slice_fusion.1
  59.9 0.0 collective-permute-done.3
  59.9 2.4 constant_dynamic-update-slice_fusion
  62.3 8.0 %gather_fusion = bf16[64,2,128,256]{3,2,1,0:T(8,128)(2,1)} fusion(bf16[40,2,128,256]{3,2,1,0:T(8,128)(2,1)} %constant_dynamic-update-slice_fusion, s32[1024]{0:T(1024)S(1)} %pad_clamp_fusion), kind=kCustom, calls=%fused_computation | custom fusion | bytes 16777472 | tf_op jit(solution)/shard_map/gather | solution.py:63
  70.3 3.8 %fusion.40 = (bf16[8,8,2,128,128]{4,3,2,1,0:T(8,128)(2,1)S(1)}, bf16[8,8,2,128,128]{4,3,2,1,0:T(8,128)(2,1)S(1)}) fusion(bf16[8,8,2,128,256]{4,3,2,1,0:T(8,128)(2,1)} %bitcast.53), kind=kLoop, calls=%fused_computation.64 | loop fusion | bytes 16777216 | tf_op jit(solution)/shard_map/slice | solution.py:67
  74.1 2.4 fusion
  76.5 2.0 fusion.1
  78.5 0.0 copy-start.5
  78.5 2.8 %fusion.26 = bf16[2,8,128,128]{2,3,1,0:T(8,128)(2,1)S(1)} fusion(bf16[8,8,2,128,128]{4,3,2,1,0:T(8,128)(2,1)S(1)} %get-tuple-element.5, f32[8,2,128,8,128]{2,4,3,1,0:T(8,128)S(1)} %get-tuple-element.14, f32[8,2,128]{2,1,0:T(2,128)S(1)} %fusion.1, f32[8,2,128]{2,1,0:T(2,128)S(1)} %get-tuple-element.13, pred[8,8]{1,0:T(8,128)(4,1)S(1)} %iota_compare_fusion), kind=kOutput, calls=%fused_computation.34 | convolution fusion | flops 547618816 | bytes 13123648 | tf_op jit(solution)/shard_map/bshqjk,bjskhe->sbqhe/dot_general | solution.py:78
  81.3 0.0 copy-done.5
  81.3 2.1 convolution_convert_fusion
  83.4 0.0 all-gather.3.cloned.1.call-update
  83.4 0.3 reduce-scatter.4.cloned.1.call-start
  83.7 90.1 %all-gather.3.cloned.1.call-done = bf16[8,1024,512]{2,1,0:T(8,128)(2,1)} async-done(((bf16[2,1024,512]{2,1,0:T(8,128)(2,1)}), bf16[8,1024,512]{2,1,0:T(8,128)(2,1)}) %all-gather.3.cloned.1.call-update) | async-done | bytes 8388624 | tf_op jit(solution)/shard_map/all_gather | solution.py:85
  173.8 6.7 %reduce_sum.60 = bf16[2,1024,512]{2,1,0:T(8,128)(2,1)} reduce(bf16[4,2,1024,512]{3,2,1,0:T(8,128)(2,1)} %bitcast.54, bf16[]{:T(256)} %constant.53.clone.1), dimensions={0}, to_apply=%region_4.5 | reduce | flops 3145728 | bytes 10485762 | tf_op jit(solution)/shard_map/reduce_sum | solution.py:85
  180.5 4.2 %convert_add_fusion = (f32[2,1024,512]{2,1,0:T(8,128)}, f32[2,1024]{1,0:T(2,128)S(1)}) fusion(bf16[2,1024,512]{2,1,0:T(8,128)(2,1)S(1)} %copy-done.1, bf16[2,1024,512]{2,1,0:T(8,128)(2,1)} %reduce_sum.60), kind=kLoop, calls=%fused_computation.6 | loop fusion | flops 4192256 | bytes 8396800 | tf_op jit(solution)/shard_map/add | solution.py:88
  184.7 0.0 copy-done.2
  184.7 1.0 multiply_reduce_fusion
  185.7 0.0 copy-done
  185.7 0.0 copy-done.9
  185.7 5.5 %fusion.19 = bf16[2,1024,512]{2,1,0:T(8,128)(2,1)} fusion(f32[2,512]{1,0:T(2,128)S(1)} %get-tuple-element.12, f32[2,512]{1,0:T(2,128)S(1)} %get-tuple-element.15, f32[2,1024]{1,0:T(2,128)S(1)} %add_rsqrt_fusion, f32[2,1024]{1,0:T(2,128)S(1)} %broadcast_multiply_fusion, bf16[512,512]{1,0:T(8,128)(2,1)S(1)} %copy-done, bf16[512,512]{1,0:T(8,128)(2,1)S(1)} %copy-done.9, ...), kind=kOutput, calls=%fused_computation.29 | convolution fusion | flops 2162163712 | bytes 7364608 | tf_op jit(solution)/shard_map/srf,fd->srd/dot_general | solution.py:95
  191.2 5.0 %copy.48 = bf16[2,1024,512]{1,0,2:T(2,128)(2,1)S(1)} copy(bf16[2,1024,512]{2,1,0:T(8,128)(2,1)} %fusion.19) | data formatting | bytes 4194304
  196.2 1.9 copy.52
  198.2 0.0 reduce-scatter.4.cloned.1.call-update
  198.2 33.4 %reduce-scatter.4.cloned.1.call-done = bf16[128,2048]{1,0:T(8,128)(2,1)} async-done(((bf16[512,2048]{1,0:T(8,128)(2,1)}), bf16[128,2048]{1,0:T(8,128)(2,1)}) %reduce-scatter.4.cloned.1.call-update) | async-done | bytes 524304
  231.7 1.4 reshape.112
  233.1 0.5 copy.49
  233.6 2.1 add_convert_fusion.6
  (9 shorter events, 0.1 us)
Async XLA Ops:
  6.5 179.2 %copy-start = (bf16[512,512]{1,0:T(8,128)(2,1)S(1)}, bf16[512,512]{1,0:T(8,128)(2,1)}, u32[]{:S(2)}) copy-start(bf16[512,512]{1,0:T(8,128)(2,1)} %param.15) | copy-start | bytes 1572868
  6.5 4.7 %copy-start.1 = (bf16[2,1024,512]{2,1,0:T(8,128)(2,1)S(1)}, bf16[2,1024,512]{2,1,0:T(8,128)(2,1)}, u32[]{:S(2)}) copy-start(bf16[2,1024,512]{2,1,0:T(8,128)(2,1)} %param.9) | copy-start | bytes 6291460
  6.5 4.6 %copy-start.6 = (f32[2,2,512]{2,1,0:T(2,128)S(1)}, f32[2,2,512]{2,1,0:T(2,128)}, u32[]{:S(2)}) copy-start(f32[2,2,512]{2,1,0:T(2,128)} %param.11) | copy-start | bytes 24580
  6.5 4.6 %copy-start.7 = (f32[2,2,512]{2,1,0:T(2,128)S(1)}, f32[2,2,512]{2,1,0:T(2,128)}, u32[]{:S(2)}) copy-start(f32[2,2,512]{2,1,0:T(2,128)} %param.10) | copy-start | bytes 24580
  6.5 5.6 %copy-start.10 = (bf16[512,3,128]{2,0,1:T(8,128)(2,1)S(1)}, bf16[512,3,128]{2,0,1:T(8,128)(2,1)}, u32[]{:S(2)}) copy-start(bf16[512,3,128]{2,0,1:T(8,128)(2,1)} %param.12) | copy-start | bytes 1179652
  6.5 167.2 %all-gather.3.cloned.1.call-start = ((), (), s32[]{:S(2)}) async-start(), calls=%async_computation.1 | async-start | bytes 10485760 | tf_op jit(solution)/shard_map/all_gather | solution.py:85
  12.2 14.9 %copy-start.8 = (s32[8,8]{1,0:T(8,128)S(1)}, s32[8,8]{1,0:T(8,128)}, u32[]{:S(2)}) copy-start(s32[8,8]{1,0:T(8,128)} %param.16) | copy-start | bytes 772
  12.2 15.0 %copy-start.11 = (s32[8]{0:T(128)S(1)}, s32[8]{0:T(128)}, u32[]{:S(2)}) copy-start(s32[8]{0:T(128)} %param.17) | copy-start | bytes 100
  13.2 1.2 copy-start.4
  17.7 31.8 %collective-permute-start = (bf16[8,2,128,256]{3,2,1,0:T(8,128)(2,1)}, bf16[8,2,128,256]{3,2,1,0:T(8,128)(2,1)}, u32[]{:S(2)}, u32[]{:S(2)}) collective-permute-start(bf16[8,2,128,256]{3,2,1,0:T(8,128)(2,1)} %copy.30), channel_id=1, source_target_pairs={{248,0},{252,4},{0,8},{4,12},{8,16},{12,20},{16,24},{20,28},{24,32... | collective-permute-start | bytes 3145736 | tf_op jit(solution)/shard_map/ppermute | solution.py:28
  19.8 34.5 %collective-permute-start.1 = (bf16[8,2,128,256]{3,2,1,0:T(8,128)(2,1)}, bf16[8,2,128,256]{3,2,1,0:T(8,128)(2,1)}, u32[]{:S(2)}, u32[]{:S(2)}) collective-permute-start(bf16[8,2,128,256]{3,2,1,0:T(8,128)(2,1)} %copy.30), channel_id=1, source_target_pairs={{0,4},{4,8},{8,12},{12,16},{16,20},{20,24},{24,28},{28,32},{32,36}... | collective-permute-start | bytes 3145736 | tf_op jit(solution)/shard_map/ppermute | solution.py:19
  21.8 35.8 %collective-permute-start.2 = (bf16[8,2,128,256]{3,2,1,0:T(8,128)(2,1)}, bf16[8,2,128,256]{3,2,1,0:T(8,128)(2,1)}, u32[]{:S(2)}, u32[]{:S(2)}) collective-permute-start(bf16[8,2,128,256]{3,2,1,0:T(8,128)(2,1)} %copy.30), channel_id=1, source_target_pairs={{4,0},{8,4},{12,8},{16,12},{20,16},{24,20},{28,24},{32,28},{36,32}... | collective-permute-start | bytes 3145736 | tf_op jit(solution)/shard_map/ppermute | solution.py:20
  21.8 38.1 %collective-permute-start.3 = (bf16[8,2,128,256]{3,2,1,0:T(8,128)(2,1)}, bf16[8,2,128,256]{3,2,1,0:T(8,128)(2,1)}, u32[]{:S(2)}, u32[]{:S(2)}) collective-permute-start(bf16[8,2,128,256]{3,2,1,0:T(8,128)(2,1)} %copy.30), channel_id=1, source_target_pairs={{8,0},{12,4},{16,8},{20,12},{24,16},{28,20},{32,24},{36,28},{40,32... | collective-permute-start | bytes 3145736 | tf_op jit(solution)/shard_map/ppermute | solution.py:28
  27.2 29.4 %copy-start.3 = (bf16[8,2,128,256]{3,2,1,0:T(8,128)(2,1)S(1)}, bf16[8,2,128,256]{3,2,1,0:T(8,128)(2,1)}, u32[]{:S(2)}) copy-start(bf16[8,2,128,256]{3,2,1,0:T(8,128)(2,1)} %copy.30) | copy-start | bytes 3145732
  78.5 2.8 %copy-start.5 = (bf16[128,512]{1,0:T(8,128)(2,1)S(1)}, bf16[128,512]{1,0:T(8,128)(2,1)}, u32[]{:S(2)}) copy-start(bf16[128,512]{1,0:T(8,128)(2,1)} %param.13) | copy-start | bytes 393220
  83.4 148.3 %reduce-scatter.4.cloned.1.call-start = ((), (), s32[]{:S(2)}) async-start(), calls=%async_computation.2 | async-start | bytes 2621440
  180.5 4.2 %copy-start.2 = (bf16[2,1024,512]{2,1,0:T(8,128)(2,1)S(1)}, bf16[2,1024,512]{2,1,0:T(8,128)(2,1)}, u32[]{:S(2)}) copy-start(bf16[2,1024,512]{2,1,0:T(8,128)(2,1)} %reduce_sum.60) | copy-start | bytes 6291460
  184.7 1.0 copy-start.9
Sparse Core Ops, SparseCore 0:
  83.5 90.2 all-gather.2
  198.3 33.2 reduce-scatter.3
